TPU v7x, 128 devices: a whole 4x4x4 slice. The times are simulated.
128 devices in a mesh: grp: 8 (over z_lo, x), shard: 16 (over y, z_hi, core).
Axes of the slice: x: 4, y: 4, z: 4 (z_hi: 2, z_lo: 2; z = z_hi * 2 + z_lo), core: 2. Of those that a mesh axis runs over, the one named last changes fastest.
Arguments:
- amplitudes: float32 [1024, 65536], P(None, 'shard'), may hold values from -6 to 6
- integrals: float32 [8192, 65536], P('grp', 'shard'), may hold values from -0.0234375 to 0.0234375
- cycle_inter: float32 [8192, 8192], P('shard', 'grp'), may hold values from -0.0625 to 0.0625
Outputs:
- cycle_out: float32 [1024, 8192], P('shard', 'grp')
All inputs are finite; a program needn't handle non-finite values.
Results may differ from a plain program's by a relative error of at most 0.000076.
Values sent between devices are 32-bit elements; how exact they have to be, the bound alone decides.
No kernel may reach another device: no remote copies, remote signals or barrier semaphores. Data moves between devices by JAX's collectives and lax.ppermute only.
A program may use at most 128 MiB of HBM per device.

v0:
```python
import functools

import jax
import jax.numpy as jnp
from jax import lax
from jax.experimental import pallas as pl
from jax.experimental.pallas import tpu as pltpu
from jax.sharding import Mesh, PartitionSpec as P

AXES = ("zl", "x", "y", "zh", "c")
C = 256
O = 32
DEPTH = 512
SLOTS = 2
SWAP = ((0, 1), (1, 0))


def halves(x):
    high = x.astype(jnp.bfloat16)
    return high, (x - high.astype(jnp.float32)).astype(jnp.bfloat16)


def product(a, b, dims):
    (a_high, a_low), (b_high, b_low) = a, b
    run = functools.partial(
        lax.dot_general, dimension_numbers=(dims, ((), ())), preferred_element_type=jnp.float32
    )
    return run(a_high, b_high) + run(a_low, b_high) + run(a_high, b_low)


def ladder_kernel(h, core_ref, v_hbm, t_hbm, far_ref, own_ref, t_held, v_held, t_sem, v_sem):
    slots, rows, core = t_held.shape[0], C, core_ref[0]
    steps = t_hbm.shape[1] // DEPTH
    starts = (2 - 2 * core + h, 2 * core + h)

    def copies(k):
        columns, slot = pl.ds(pl.multiple_of(k * DEPTH, DEPTH), DEPTH), lax.rem(k, slots)
        made = [pltpu.make_async_copy(t_hbm.at[:, columns], t_held.at[slot], t_sem.at[slot])]
        for side, start in enumerate(starts):
            made.append(
                pltpu.make_async_copy(
                    v_hbm.at[pl.ds(pl.multiple_of(start * rows, rows), rows), columns],
                    v_held.at[slot, pl.ds(side * rows, rows)],
                    v_sem.at[slot, side],
                )
            )
        return made

    for k in range(slots - 1):
        for copy in copies(jnp.int32(k)):
            copy.start()
    far_ref[...] = jnp.zeros_like(far_ref)
    own_ref[...] = jnp.zeros_like(own_ref)

    def step(k, _):
        for copy in copies(k):
            copy.wait()

        @pl.when(k + slots - 1 < steps)
        def _():
            for copy in copies(k + slots - 1):
                copy.start()

        slot = lax.rem(k, slots)
        part = product(halves(v_held[slot]), halves(t_held[slot]), ((1,), (1,)))
        far_ref[...] += part[:rows]
        own_ref[...] += part[rows:]
        return 0

    lax.fori_loop(0, steps, step, 0)


def ladder(core, integrals, amplitudes, h):
    ef, pairs = integrals.shape[1], amplitudes.shape[0]
    vmem, hbm = pl.BlockSpec(memory_space=pltpu.VMEM), pl.BlockSpec(memory_space=pl.ANY)
    return pl.pallas_call(
        functools.partial(ladder_kernel, h),
        out_shape=[jax.ShapeDtypeStruct((C, pairs), jnp.float32)] * 2,
        in_specs=[pl.BlockSpec(memory_space=pltpu.SMEM), hbm, hbm],
        out_specs=[vmem] * 2,
        scratch_shapes=[
            pltpu.VMEM((SLOTS, pairs, DEPTH), jnp.float32),
            pltpu.VMEM((SLOTS, 2 * C, DEPTH), jnp.float32),
            pltpu.SemaphoreType.DMA((SLOTS,)),
            pltpu.SemaphoreType.DMA((SLOTS, 2)),
        ],
        compiler_params=pltpu.CompilerParams(vmem_limit_bytes=52 * 1024 * 1024),
        cost_estimate=pl.CostEstimate(
            flops=12 * C * pairs * ef,
            bytes_accessed=4 * ef * (2 * C + pairs),
            transcendentals=0,
        ),
    )(core, integrals, amplitudes)


def cycle_kernel(place_ref, own_rows, rows1, rows2, rows3, w_own, w_far, out_ref, *scratch):
    half = w_own.shape[0]

    @pl.when(pl.program_id(0) == 0)
    def _():
        for step, rows in enumerate((own_rows, rows1, rows2, rows3)):
            for other in range(2):
                to = pl.ds(pl.multiple_of(place_ref[2 * step + other] * O, O), O)
                for side in range(2):
                    start = pl.multiple_of(place_ref[8 + side] * half, half)
                    high, low = halves(rows[other, :, pl.ds(start, half)])
                    scratch[2 * side][to, :] = high
                    scratch[2 * side + 1][to, :] = low

    own = (scratch[0][...], scratch[1][...])
    far = (scratch[2][...], scratch[3][...])
    out_ref[...] = product(own, halves(w_own[...]), ((1,), (0,))) + product(
        far, halves(w_far[...]), ((1,), (0,))
    )


def cycle(place, rows, w_own, w_far):
    half, columns = w_own.shape
    wide = 256
    whole = pl.BlockSpec(rows[0].shape, lambda n, place: (0, 0, 0))
    panel = pl.BlockSpec((half, wide), lambda n, place: (0, n))
    return pl.pallas_call(
        cycle_kernel,
        out_shape=jax.ShapeDtypeStruct((8 * O, columns), jnp.float32),
        grid_spec=pltpu.PrefetchScalarGridSpec(
            num_scalar_prefetch=1,
            grid=(columns // wide,),
            in_specs=[whole] * 4 + [panel] * 2,
            out_specs=pl.BlockSpec((8 * O, wide), lambda n, place: (0, n)),
            scratch_shapes=[pltpu.VMEM((8 * O, half), jnp.bfloat16)] * 4,
        ),
        compiler_params=pltpu.CompilerParams(
            dimension_semantics=("arbitrary",), vmem_limit_bytes=24 * 1024 * 1024
        ),
        cost_estimate=pl.CostEstimate(
            flops=6 * 8 * O * 2 * half * columns,
            bytes_accessed=4 * (2 * half * columns + 8 * O * (2 * half + columns)),
            transcendentals=0,
        ),
    )(place, *rows, w_own, w_far)


def regroup_kernel(got_ref, out_ref, held):
    blocks, rows, columns = got_ref.shape
    total = got_ref[0]
    for n in range(1, blocks):
        total = total + got_ref[n]
    for i in range(columns // O):
        held[i] = total[:, i * O : (i + 1) * O]
    for c in range(rows):
        out_ref[:, c * O : (c + 1) * O] = held[:, c, :]


def finish_kernel(done_ref, got_ref, out_ref):
    rows = done_ref.shape[0]
    total = got_ref[0]
    for n in range(1, got_ref.shape[0]):
        total = total + got_ref[n]
    out_ref[:rows, :] = done_ref[...]
    out_ref[rows:, :] = total


def small(kernel, shape, scratch, *args):
    vmem = pl.BlockSpec(memory_space=pltpu.VMEM)
    size = 4 * sum(a.size for a in args)
    return pl.pallas_call(
        kernel,
        out_shape=jax.ShapeDtypeStruct(shape, jnp.float32),
        in_specs=[vmem] * len(args),
        out_specs=vmem,
        scratch_shapes=scratch,
        compiler_params=pltpu.CompilerParams(vmem_limit_bytes=8 * 1024 * 1024),
        cost_estimate=pl.CostEstimate(flops=size, bytes_accessed=size, transcendentals=0),
    )(*args)


def scatter(x):
    return lax.all_to_all(x, ("y", "zh"), 0, 0)


def shards(amplitudes, integrals, cycle_inter):
    core, x, zl = (lax.axis_index(name).astype(jnp.int32) for name in ("c", "x", "zl"))
    place = jnp.stack(
        [(zl + other) % 2 * 4 + (x + 4 - step) % 4 for step in range(4) for other in range(2)]
        + [core, 1 - core]
    )
    other = lax.ppermute(cycle_inter, "c", SWAP)
    near, kept = [], []
    for h in range(2):
        far_block, own_block = ladder(core.reshape(1), integrals, amplitudes, h)
        near.append(lax.ppermute(far_block, "c", SWAP))
        kept.append(own_block)
    got = []
    for h in range(2):
        block = scatter((kept[h] + near[h]).reshape(8, C // 8, O * O))
        mine = small(
            regroup_kernel, (O, C // 8 * O), [pltpu.VMEM((O, C // 8, O), jnp.float32)], block
        )
        far = lax.ppermute(mine, "zl", SWAP)
        pair = jnp.stack([mine, far])
        rows = [pair]
        for step in (1, 2, 3):
            rows.append(lax.ppermute(pair, "x", [(i, (i + step) % 4) for i in range(4)]))
        part = cycle(place, rows, cycle_inter, other)
        got.append(scatter(part.reshape(8, O, part.shape[1])))
    return small(finish_kernel, (2 * O, got[1].shape[2]), [], jnp.sum(got[0], 0), got[1])


def solution(mesh):
    fine = Mesh(mesh.devices.reshape(2, 4, 4, 2, 2), AXES)
    group, shard = ("zl", "x"), ("y", "zh", "c")
    return jax.shard_map(
        shards,
        mesh=fine,
        in_specs=(P(None, shard), P(group, shard), P(shard, group)),
        out_specs=P(shard, group),
        check_vma=False,
    )
```

profile of v0, /device:TPU:0, one launch (start us, length us, event | category | flops | bytes accessed | tf_op | source)
XLA Modules:
  0.0 174.1 jit_solution(16622987296044559222)
XLA Ops:
  0.0 0.0 copy-start
  0.0 17.8 %shard_map.37 = (f32[256,1024]{1,0:T(8,128)S(1)}, f32[256,1024]{1,0:T(8,128)}) custom-call(s32[1]{0:T(128)} %bitcast.8.core_ref, f32[1024,4096]{1,0:T(8,128)} %v_hbm.3, f32[1024,4096]{1,0:T(8,128)} %t_hbm.3), custom_call_target="tpu_custom_call" | custom-call | flops 12884901888 | bytes 25165824 | tf_op jit(solution)/shard_map/pallas_call | solution.py:76
  17.8 0.0 copy-start.3
  17.8 0.1 collective-permute-start
  17.9 0.0 copy-done
  17.9 0.5 collective-permute-start.5
  18.4 17.9 %shard_map.40 = (f32[256,1024]{1,0:T(8,128)}, f32[256,1024]{1,0:T(8,128)}) custom-call(s32[1]{0:T(128)} %bitcast.8.core_ref, f32[1024,4096]{1,0:T(8,128)} %v_hbm.3, f32[1024,4096]{1,0:T(8,128)} %t_hbm.3), custom_call_target="tpu_custom_call" | custom-call | flops 12884901888 | bytes 25165824 | tf_op jit(solution)/shard_map/pallas_call | solution.py:76
  36.3 0.2 collective-permute-start.6
  36.5 0.0 collective-permute-done
  36.5 0.0 copy-done.3
  36.5 1.2 add.100
  37.6 7.9 %all-to-all-start = ((f32[8,32,1024]{2,1,0:T(8,128)}), f32[8,32,1024]{2,1,0:T(8,128)S(1)}, u32[]{:S(2)}, u32[]{:S(2)}) async-start(f32[8,32,1024]{2,1,0:T(8,128)} %bitcast.21), calls=%async_computation | async-start | bytes 2097152 | tf_op jit(solution)/shard_map/all_to_all | solution.py:178
  45.5 0.0 collective-permute-done.6
  45.5 2.7 %add.101 = f32[256,1024]{1,0:T(8,128)} add(f32[256,1024]{1,0:T(8,128)} %get-tuple-element.11, f32[256,1024]{1,0:T(8,128)} %collective-permute-done.6) | non-fusion elementwise | flops 262144 | bytes 3145728 | tf_op jit(solution)/shard_map/add | solution.py:195
  48.2 14.4 %all-to-all-done.got_ref = f32[8,32,1024]{2,1,0:T(8,128)S(1)} async-done(((f32[8,32,1024]{2,1,0:T(8,128)}), f32[8,32,1024]{2,1,0:T(8,128)S(1)}, u32[]{:S(2)}, u32[]{:S(2)}) %all-to-all-start) | async-done | bytes 1048608 | tf_op jit(solution)/shard_map/all_to_all | solution.py:178
  62.6 0.0 copy-start.1
  62.7 1.0 copy-done.1
  63.6 3.6 %all-to-all-start.2 = ((f32[8,32,1024]{2,1,0:T(8,128)}), f32[8,32,1024]{2,1,0:T(8,128)S(1)}, u32[]{:S(2)}, u32[]{:S(2)}) async-start(f32[8,32,1024]{2,1,0:T(8,128)} %bitcast.20), calls=%async_computation.2 | async-start | bytes 2097152 | tf_op jit(solution)/shard_map/all_to_all | solution.py:178
  67.2 0.0 copy-start.2
  67.2 1.2 copy-done.2
  68.4 0.4 shard_map.38
  68.8 1.1 collective-permute-start.1
  69.9 12.7 %collective-permute-done.1 = f32[32,1024]{1,0:T(8,128)S(1)} collective-permute-done((f32[32,1024]{1,0:T(8,128)S(1)}, f32[32,1024]{1,0:T(8,128)S(1)}, u32[]{:S(2)}, u32[]{:S(2)}) %collective-permute-start.1) | collective-permute-done | bytes 131104 | tf_op jit(solution)/shard_map/ppermute | solution.py:199
  82.7 2.8 %collective-permute-start.4 = (f32[2,32,1024]{2,1,0:T(8,128)S(1)}, f32[2,32,1024]{2,1,0:T(8,128)}, u32[]{:S(2)}, u32[]{:S(2)}) collective-permute-start(f32[2,32,1024]{2,1,0:T(8,128)S(1)} %pad_maximum_fusion.own_rows), channel_id=1, source_target_pairs={{0,48},{16,0},{32,16},{48,32},{1,49},{17,1},{33,17},{49,33},{2,50}... | collective-permute-start | bytes 786440 | tf_op jit(solution)/shard_map/ppermute | solution.py:203
  85.5 0.8 collective-permute-start.3
  86.3 0.9 collective-permute-start.2
  87.2 0.1 stack.61.place_ref
  87.3 0.0 collective-permute-done.5.w_far
  87.3 8.2 %collective-permute-done.4.rows3 = f32[2,32,1024]{2,1,0:T(8,128)} collective-permute-done((f32[2,32,1024]{2,1,0:T(8,128)S(1)}, f32[2,32,1024]{2,1,0:T(8,128)}, u32[]{:S(2)}, u32[]{:S(2)}) %collective-permute-start.4) | collective-permute-done | bytes 262176 | tf_op jit(solution)/shard_map/ppermute | solution.py:203
  95.5 0.8 collective-permute-done.3.rows2
  96.3 3.0 %collective-permute-done.2.rows1 = f32[2,32,1024]{2,1,0:T(8,128)} collective-permute-done((f32[2,32,1024]{2,1,0:T(8,128)S(1)}, f32[2,32,1024]{2,1,0:T(8,128)}, u32[]{:S(2)}, u32[]{:S(2)}) %collective-permute-start.2) | collective-permute-done | bytes 262176 | tf_op jit(solution)/shard_map/ppermute | solution.py:203
  99.2 5.7 %shard_map.39 = f32[256,1024]{1,0:T(8,128)} custom-call(s32[10]{0:T(128)S(1)} %stack.61.place_ref, f32[2,32,1024]{2,1,0:T(8,128)S(1)} %pad_maximum_fusion.own_rows, f32[2,32,1024]{2,1,0:T(8,128)} %collective-permute-done.2.rows1, f32[2,32,1024]{2,1,0:T(8,128)} %collective-permute-done.3.rows2, f32[2,32,1024]{2,1,0:T(8,128)} %collective-permute-done.4.rows3, ...), custom_call_target="tpu_custom_call" | custom-call | flops 1610612736 | bytes 6291456 | tf_op jit(solution)/shard_map/pallas_call | solution.py:122
  105.0 0.0 all-to-all-done.2.got_ref
  105.0 8.9 %all-to-all-start.1 = ((f32[8,32,1024]{2,1,0:T(8,128)}), f32[8,32,1024]{2,1,0:T(8,128)}, u32[]{:S(2)}, u32[]{:S(2)}) async-start(f32[8,32,1024]{2,1,0:T(8,128)} %bitcast.13), calls=%async_computation.1 | async-start | bytes 2097152 | tf_op jit(solution)/shard_map/all_to_all | solution.py:178
  113.9 0.4 shard_map.41
  114.3 0.1 collective-permute-start.7
  114.4 14.2 %collective-permute-done.7 = f32[32,1024]{1,0:T(8,128)S(1)} collective-permute-done((f32[32,1024]{1,0:T(8,128)S(1)}, f32[32,1024]{1,0:T(8,128)S(1)}, u32[]{:S(2)}, u32[]{:S(2)}) %collective-permute-start.7) | collective-permute-done | bytes 131104 | tf_op jit(solution)/shard_map/ppermute | solution.py:199
  128.5 0.1 collective-permute-start.10
  128.6 0.9 collective-permute-start.9
  129.5 1.3 collective-permute-start.8
  130.8 7.0 %collective-permute-done.10.rows3 = f32[2,32,1024]{2,1,0:T(8,128)S(1)} collective-permute-done((f32[2,32,1024]{2,1,0:T(8,128)S(1)}, f32[2,32,1024]{2,1,0:T(8,128)S(1)}, u32[]{:S(2)}, u32[]{:S(2)}) %collective-permute-start.10) | collective-permute-done | bytes 262176 | tf_op jit(solution)/shard_map/ppermute | solution.py:203
  137.8 1.6 collective-permute-done.9.rows2
  139.4 3.8 %collective-permute-done.8.rows1 = f32[2,32,1024]{2,1,0:T(8,128)S(1)} collective-permute-done((f32[2,32,1024]{2,1,0:T(8,128)S(1)}, f32[2,32,1024]{2,1,0:T(8,128)S(1)}, u32[]{:S(2)}, u32[]{:S(2)}) %collective-permute-start.8) | collective-permute-done | bytes 262176 | tf_op jit(solution)/shard_map/ppermute | solution.py:203
  143.2 5.5 %shard_map.42 = f32[256,1024]{1,0:T(8,128)} custom-call(s32[10]{0:T(128)S(1)} %stack.61.place_ref, f32[2,32,1024]{2,1,0:T(8,128)S(1)} %pad_maximum_fusion.1.own_rows, f32[2,32,1024]{2,1,0:T(8,128)S(1)} %collective-permute-done.8.rows1, f32[2,32,1024]{2,1,0:T(8,128)S(1)} %collective-permute-done.9.rows2, f32[2,32,1024]{2,1,0:T(8,128)S(1)} %collective-permute-done.10.rows3, ...), custom_call_target="tpu_custom_call" | custom-call | flops 1610612736 | bytes 6291456 | tf_op jit(solution)/shard_map/pallas_call | solution.py:122
  148.7 0.0 all-to-all-done.1
  148.7 8.4 %all-to-all-start.3 = ((f32[8,32,1024]{2,1,0:T(8,128)}), f32[8,32,1024]{2,1,0:T(8,128)S(1)}, u32[]{:S(2)}, u32[]{:S(2)}) async-start(f32[8,32,1024]{2,1,0:T(8,128)} %bitcast.17), calls=%async_computation.3 | async-start | bytes 2097152 | tf_op jit(solution)/shard_map/all_to_all | solution.py:178
  157.1 1.3 reduce_sum.9.done_ref
  158.4 15.0 %all-to-all-done.3.got_ref = f32[8,32,1024]{2,1,0:T(8,128)S(1)} async-done(((f32[8,32,1024]{2,1,0:T(8,128)}), f32[8,32,1024]{2,1,0:T(8,128)S(1)}, u32[]{:S(2)}, u32[]{:S(2)}) %all-to-all-start.3) | async-done | bytes 1048608 | tf_op jit(solution)/shard_map/all_to_all | solution.py:178
  173.4 0.8 shard_map.43
  (2 shorter events, 0.0 us)
Async XLA Ops:
  0.0 17.9 %copy-start = (f32[512,1024]{1,0:T(8,128)S(1)}, f32[512,1024]{1,0:T(8,128)}, u32[]{:S(2)}) copy-start(f32[512,1024]{1,0:T(8,128)} %w_own.3) | copy-start | bytes 6291460
  17.8 18.7 %copy-start.3 = (f32[256,1024]{1,0:T(8,128)S(1)}, f32[256,1024]{1,0:T(8,128)}, u32[]{:S(2)}) copy-start(f32[256,1024]{1,0:T(8,128)} %get-tuple-element.9) | copy-start | bytes 3145732
  17.8 18.6 %collective-permute-start = (f32[256,1024]{1,0:T(8,128)S(1)}, f32[256,1024]{1,0:T(8,128)S(1)}, u32[]{:S(2)}, u32[]{:S(2)}) collective-permute-start(f32[256,1024]{1,0:T(8,128)S(1)} %get-tuple-element.10), channel_id=1, source_target_pairs={{0,1},{1,0},{2,3},{3,2},{4,5},{5,4},{6,7},{7,6},{8,9},{9,8},{10,11... | collective-permute-start | bytes 3145736 | tf_op jit(solution)/shard_map/ppermute | solution.py:191
  17.9 69.4 %collective-permute-start.5 = (f32[512,1024]{1,0:T(8,128)S(1)}, f32[512,1024]{1,0:T(8,128)}, u32[]{:S(2)}, u32[]{:S(2)}) collective-permute-start(f32[512,1024]{1,0:T(8,128)S(1)} %copy-done), channel_id=1, source_target_pairs={{0,1},{1,0},{2,3},{3,2},{4,5},{5,4},{6,7},{7,6},{8,9},{9,8},{10,11... | collective-permute-start | bytes 6291464 | tf_op jit(solution)/shard_map/ppermute | solution.py:187
  36.3 9.3 %collective-permute-start.6 = (f32[256,1024]{1,0:T(8,128)}, f32[256,1024]{1,0:T(8,128)}, u32[]{:S(2)}, u32[]{:S(2)}) collective-permute-start(f32[256,1024]{1,0:T(8,128)} %get-tuple-element.12), channel_id=1, source_target_pairs={{0,1},{1,0},{2,3},{3,2},{4,5},{5,4},{6,7},{7,6},{8,9},{9,8},{10,11... | collective-permute-start | bytes 3145736 | tf_op jit(solution)/shard_map/ppermute | solution.py:191
  37.6 25.0 %all-to-all-start = ((f32[8,32,1024]{2,1,0:T(8,128)}), f32[8,32,1024]{2,1,0:T(8,128)S(1)}, u32[]{:S(2)}, u32[]{:S(2)}) async-start(f32[8,32,1024]{2,1,0:T(8,128)} %bitcast.21), calls=%async_computation | async-start | bytes 2097152 | tf_op jit(solution)/shard_map/all_to_all | solution.py:178
  62.6 1.0 copy-start.1
  63.6 41.4 %all-to-all-start.2 = ((f32[8,32,1024]{2,1,0:T(8,128)}), f32[8,32,1024]{2,1,0:T(8,128)S(1)}, u32[]{:S(2)}, u32[]{:S(2)}) async-start(f32[8,32,1024]{2,1,0:T(8,128)} %bitcast.20), calls=%async_computation.2 | async-start | bytes 2097152 | tf_op jit(solution)/shard_map/all_to_all | solution.py:178
  67.2 1.2 copy-start.2
  68.8 13.8 %collective-permute-start.1 = (f32[32,1024]{1,0:T(8,128)S(1)}, f32[32,1024]{1,0:T(8,128)S(1)}, u32[]{:S(2)}, u32[]{:S(2)}) collective-permute-start(f32[32,1024]{1,0:T(8,128)S(1)} %shard_map.38), channel_id=1, source_target_pairs={{0,64},{64,0},{1,65},{65,1},{2,66},{66,2},{3,67},{67,3},{4,68},{68... | collective-permute-start | bytes 393224 | tf_op jit(solution)/shard_map/ppermute | solution.py:199
  82.7 12.8 %collective-permute-start.4 = (f32[2,32,1024]{2,1,0:T(8,128)S(1)}, f32[2,32,1024]{2,1,0:T(8,128)}, u32[]{:S(2)}, u32[]{:S(2)}) collective-permute-start(f32[2,32,1024]{2,1,0:T(8,128)S(1)} %pad_maximum_fusion.own_rows), channel_id=1, source_target_pairs={{0,48},{16,0},{32,16},{48,32},{1,49},{17,1},{33,17},{49,33},{2,50}... | collective-permute-start | bytes 786440 | tf_op jit(solution)/shard_map/ppermute | solution.py:203
  85.5 10.8 %collective-permute-start.3 = (f32[2,32,1024]{2,1,0:T(8,128)S(1)}, f32[2,32,1024]{2,1,0:T(8,128)}, u32[]{:S(2)}, u32[]{:S(2)}) collective-permute-start(f32[2,32,1024]{2,1,0:T(8,128)S(1)} %pad_maximum_fusion.own_rows), channel_id=1, source_target_pairs={{0,32},{16,48},{32,0},{48,16},{1,33},{17,49},{33,1},{49,17},{2,34}... | collective-permute-start | bytes 786440 | tf_op jit(solution)/shard_map/ppermute | solution.py:203
  86.3 12.9 %collective-permute-start.2 = (f32[2,32,1024]{2,1,0:T(8,128)S(1)}, f32[2,32,1024]{2,1,0:T(8,128)}, u32[]{:S(2)}, u32[]{:S(2)}) collective-permute-start(f32[2,32,1024]{2,1,0:T(8,128)S(1)} %pad_maximum_fusion.own_rows), channel_id=1, source_target_pairs={{0,16},{16,32},{32,48},{48,0},{1,17},{17,33},{33,49},{49,1},{2,18}... | collective-permute-start | bytes 786440 | tf_op jit(solution)/shard_map/ppermute | solution.py:203
  105.0 43.7 %all-to-all-start.1 = ((f32[8,32,1024]{2,1,0:T(8,128)}), f32[8,32,1024]{2,1,0:T(8,128)}, u32[]{:S(2)}, u32[]{:S(2)}) async-start(f32[8,32,1024]{2,1,0:T(8,128)} %bitcast.13), calls=%async_computation.1 | async-start | bytes 2097152 | tf_op jit(solution)/shard_map/all_to_all | solution.py:178
  114.3 14.2 %collective-permute-start.7 = (f32[32,1024]{1,0:T(8,128)S(1)}, f32[32,1024]{1,0:T(8,128)S(1)}, u32[]{:S(2)}, u32[]{:S(2)}) collective-permute-start(f32[32,1024]{1,0:T(8,128)S(1)} %shard_map.41), channel_id=1, source_target_pairs={{0,64},{64,0},{1,65},{65,1},{2,66},{66,2},{3,67},{67,3},{4,68},{68... | collective-permute-start | bytes 393224 | tf_op jit(solution)/shard_map/ppermute | solution.py:199
  128.5 9.2 %collective-permute-start.10 = (f32[2,32,1024]{2,1,0:T(8,128)S(1)}, f32[2,32,1024]{2,1,0:T(8,128)S(1)}, u32[]{:S(2)}, u32[]{:S(2)}) collective-permute-start(f32[2,32,1024]{2,1,0:T(8,128)S(1)} %pad_maximum_fusion.1.own_rows), channel_id=1, source_target_pairs={{0,48},{16,0},{32,16},{48,32},{1,49},{17,1},{33,17},{49,33},{2,50}... | collective-permute-start | bytes 786440 | tf_op jit(solution)/shard_map/ppermute | solution.py:203
  128.6 10.8 %collective-permute-start.9 = (f32[2,32,1024]{2,1,0:T(8,128)S(1)}, f32[2,32,1024]{2,1,0:T(8,128)S(1)}, u32[]{:S(2)}, u32[]{:S(2)}) collective-permute-start(f32[2,32,1024]{2,1,0:T(8,128)S(1)} %pad_maximum_fusion.1.own_rows), channel_id=1, source_target_pairs={{0,32},{16,48},{32,0},{48,16},{1,33},{17,49},{33,1},{49,17},{2,34}... | collective-permute-start | bytes 786440 | tf_op jit(solution)/shard_map/ppermute | solution.py:203
  129.5 13.7 %collective-permute-start.8 = (f32[2,32,1024]{2,1,0:T(8,128)S(1)}, f32[2,32,1024]{2,1,0:T(8,128)S(1)}, u32[]{:S(2)}, u32[]{:S(2)}) collective-permute-start(f32[2,32,1024]{2,1,0:T(8,128)S(1)} %pad_maximum_fusion.1.own_rows), channel_id=1, source_target_pairs={{0,16},{16,32},{32,48},{48,0},{1,17},{17,33},{33,49},{49,1},{2,18}... | collective-permute-start | bytes 786440 | tf_op jit(solution)/shard_map/ppermute | solution.py:203
  148.7 24.7 %all-to-all-start.3 = ((f32[8,32,1024]{2,1,0:T(8,128)}), f32[8,32,1024]{2,1,0:T(8,128)S(1)}, u32[]{:S(2)}, u32[]{:S(2)}) async-start(f32[8,32,1024]{2,1,0:T(8,128)} %bitcast.17), calls=%async_computation.3 | async-start | bytes 2097152 | tf_op jit(solution)/shard_map/all_to_all | solution.py:178
where the time goes:
time: 175 us; the launch traced here: 174 us
  waiting for transfers between devices  80.6 us (46%)
  Pallas kernels  48.5 us (28%)
  starting transfers between devices  37.4 us (21%)
  other arithmetic  5.22 us (3%)
  local copies, waits for them, and re-layouts  2.28 us (1%)
    pallas_call x2, Pallas kernels, ladder(): pl.pallas_call(functools.partial(ladder_kernel, h), out_shape=[jax.ShapeD...  35.7 us
    all_to_all x4, waiting for transfers between devices, scatter(): return lax.all_to_all(x, ('y', 'zh'), 0, 0)  29.4 us
    all_to_all x4, starting transfers between devices, scatter(): return lax.all_to_all(x, ('y', 'zh'), 0, 0)  28.7 us
    ppermute x2, waiting for transfers between devices, shards(): far = lax.ppermute(mine, 'zl', SWAP)  26.9 us
    ppermute x6, waiting for transfers between devices, shards(): lax.ppermute(pair, 'x', [(i, (i + step) % 4) for i in range(4)])  24.3 us
    pallas_call x2, Pallas kernels, cycle(): pl.pallas_call(cycle_kernel, out_shape=jax.ShapeDtypeStruct((8 * O, colum...  11.2 us
    ppermute x6, starting transfers between devices, shards(): lax.ppermute(pair, 'x', [(i, (i + step) % 4) for i in range(4)])  6.79 us
    add x2, other arithmetic, shards(): block = scatter((kept[h] + near[h]).reshape(8, C // 8, O * O))  3.89 us
  transfers between devices with their start and end apart: 15, of which 10 were waited for; matrix products, arithmetic and copies ran while one was open for 3% of the time, Pallas kernels for 17%

commit v1 on v0

--- a/solution.py
+++ b/solution.py
@@ -93,19 +93,19 @@
     )(core, integrals, amplitudes)
 
 
-def cycle_kernel(place_ref, own_rows, rows1, rows2, rows3, w_own, w_far, out_ref, *scratch):
+def cycle_kernel(place_ref, *refs):
+    rows, (w_own, w_far, out_ref), scratch = refs[:8], refs[8:11], refs[11:]
     half = w_own.shape[0]
 
     @pl.when(pl.program_id(0) == 0)
     def _():
-        for step, rows in enumerate((own_rows, rows1, rows2, rows3)):
-            for other in range(2):
-                to = pl.ds(pl.multiple_of(place_ref[2 * step + other] * O, O), O)
-                for side in range(2):
-                    start = pl.multiple_of(place_ref[8 + side] * half, half)
-                    high, low = halves(rows[other, :, pl.ds(start, half)])
-                    scratch[2 * side][to, :] = high
-                    scratch[2 * side + 1][to, :] = low
+        for n, block in enumerate(rows):
+            to = pl.ds(pl.multiple_of(place_ref[n] * O, O), O)
+            for side in range(2):
+                start = pl.multiple_of(place_ref[8 + side] * half, half)
+                high, low = halves(block[:, pl.ds(start, half)])
+                scratch[2 * side][to, :] = high
+                scratch[2 * side + 1][to, :] = low
 
     own = (scratch[0][...], scratch[1][...])
     far = (scratch[2][...], scratch[3][...])
@@ -116,8 +116,8 @@
 
 def cycle(place, rows, w_own, w_far):
     half, columns = w_own.shape
-    wide = 256
-    whole = pl.BlockSpec(rows[0].shape, lambda n, place: (0, 0, 0))
+    wide = 512
+    whole = pl.BlockSpec(rows[0].shape, lambda n, place: (0, 0))
     panel = pl.BlockSpec((half, wide), lambda n, place: (0, n))
     return pl.pallas_call(
         cycle_kernel,
@@ -125,7 +125,7 @@
         grid_spec=pltpu.PrefetchScalarGridSpec(
             num_scalar_prefetch=1,
             grid=(columns // wide,),
-            in_specs=[whole] * 4 + [panel] * 2,
+            in_specs=[whole] * 8 + [panel] * 2,
             out_specs=pl.BlockSpec((8 * O, wide), lambda n, place: (0, n)),
             scratch_shapes=[pltpu.VMEM((8 * O, half), jnp.bfloat16)] * 4,
         ),
@@ -181,7 +181,7 @@
 def shards(amplitudes, integrals, cycle_inter):
     core, x, zl = (lax.axis_index(name).astype(jnp.int32) for name in ("c", "x", "zl"))
     place = jnp.stack(
-        [(zl + other) % 2 * 4 + (x + 4 - step) % 4 for step in range(4) for other in range(2)]
+        [(zl + other) % 2 * 4 + (x + 4 - step) % 4 for other in range(2) for step in range(4)]
         + [core, 1 - core]
     )
     other = lax.ppermute(cycle_inter, "c", SWAP)
@@ -197,10 +197,11 @@
             regroup_kernel, (O, C // 8 * O), [pltpu.VMEM((O, C // 8, O), jnp.float32)], block
         )
         far = lax.ppermute(mine, "zl", SWAP)
-        pair = jnp.stack([mine, far])
-        rows = [pair]
-        for step in (1, 2, 3):
-            rows.append(lax.ppermute(pair, "x", [(i, (i + step) % 4) for i in range(4)]))
+        rows = []
+        for block in (mine, far):
+            rows.append(block)
+            for step in (1, 2, 3):
+                rows.append(lax.ppermute(block, "x", [(i, (i + step) % 4) for i in range(4)]))
         part = cycle(place, rows, cycle_inter, other)
         got.append(scatter(part.reshape(8, O, part.shape[1])))
     return small(finish_kernel, (2 * O, got[1].shape[2]), [], jnp.sum(got[0], 0), got[1])

time: 175 us -> 162 us (0.926)
  waiting for transfers between devices: 80.6 us -> 62.5 us
  starting transfers between devices: 37.4 us -> 44 us
    ppermute x6 -> x12, waiting for transfers between devices: 24.3 us -> 13.1 us  [shards(): lax.ppermute(block, 'x', [(i, (i + step) % 4) for i in range(4)])]
    ppermute x2, waiting for transfers between devices: 26.9 us -> 20.1 us  [shards(): far = lax.ppermute(mine, 'zl', SWAP)]
    ppermute x6 -> x12, starting transfers between devices: 6.79 us -> 13.2 us  [shards(): lax.ppermute(block, 'x', [(i, (i + step) % 4) for i in range(4)])]
  transfers between devices with their start and end apart: 15 -> 21, of which waited for: 10 -> 10; matrix products, arithmetic and copies ran while one was open for 3% -> 3% of each run, Pallas kernels for 17% -> 18%
where the time goes in v1:
time: 162 us; the launch traced here: 161 us
  waiting for transfers between devices  62.5 us (39%)
  Pallas kernels  46.9 us (29%)
  starting transfers between devices  44 us (27%)
  other arithmetic  5.17 us (3%)
  local copies, waits for them, and re-layouts  2.27 us (1%)
    pallas_call x2, Pallas kernels, ladder(): pl.pallas_call(functools.partial(ladder_kernel, h), out_shape=[jax.ShapeD...  35.6 us
    all_to_all x4, waiting for transfers between devices, scatter(): return lax.all_to_all(x, ('y', 'zh'), 0, 0)  29.3 us
    all_to_all x4, starting transfers between devices, scatter(): return lax.all_to_all(x, ('y', 'zh'), 0, 0)  28.8 us
    ppermute x2, waiting for transfers between devices, shards(): far = lax.ppermute(mine, 'zl', SWAP)  20.1 us
    ppermute x12, starting transfers between devices, shards(): lax.ppermute(block, 'x', [(i, (i + step) % 4) for i in range(4)])  13.2 us
    ppermute x12, waiting for transfers between devices, shards(): lax.ppermute(block, 'x', [(i, (i + step) % 4) for i in range(4)])  13.1 us
    pallas_call x2, Pallas kernels, cycle(): pl.pallas_call(cycle_kernel, out_shape=jax.ShapeDtypeStruct((8 * O, colum...  9.71 us
    add x2, other arithmetic, shards(): block = scatter((kept[h] + near[h]).reshape(8, C // 8, O * O))  3.87 us
  transfers between devices with their start and end apart: 21, of which 10 were waited for; matrix products, arithmetic and copies ran while one was open for 3% of the time, Pallas kernels for 18%

profile of v1, /device:TPU:0, one launch (start us, length us, event | category | flops | bytes accessed | tf_op | source)
XLA Modules:
  0.0 161.0 jit_solution(8034511535025643916)
XLA Ops:
  0.0 0.0 copy-start
  0.0 17.8 %shard_map.37 = (f32[256,1024]{1,0:T(8,128)S(1)}, f32[256,1024]{1,0:T(8,128)}) custom-call(s32[1]{0:T(128)} %bitcast.8.core_ref, f32[1024,4096]{1,0:T(8,128)} %v_hbm.3, f32[1024,4096]{1,0:T(8,128)} %t_hbm.3), custom_call_target="tpu_custom_call" | custom-call | flops 12884901888 | bytes 25165824 | tf_op jit(solution)/shard_map/pallas_call | solution.py:76
  17.8 0.0 copy-start.3
  17.8 0.1 collective-permute-start
  17.9 0.0 copy-done
  17.9 0.5 collective-permute-start.8
  18.4 17.8 %shard_map.40 = (f32[256,1024]{1,0:T(8,128)}, f32[256,1024]{1,0:T(8,128)}) custom-call(s32[1]{0:T(128)} %bitcast.8.core_ref, f32[1024,4096]{1,0:T(8,128)} %v_hbm.3, f32[1024,4096]{1,0:T(8,128)} %t_hbm.3), custom_call_target="tpu_custom_call" | custom-call | flops 12884901888 | bytes 25165824 | tf_op jit(solution)/shard_map/pallas_call | solution.py:76
  36.3 0.2 collective-permute-start.9
  36.4 0.0 collective-permute-done
  36.4 0.0 copy-done.3
  36.4 1.2 add.100
  37.6 7.9 %all-to-all-start = ((f32[8,32,1024]{2,1,0:T(8,128)}), f32[8,32,1024]{2,1,0:T(8,128)S(1)}, u32[]{:S(2)}, u32[]{:S(2)}) async-start(f32[8,32,1024]{2,1,0:T(8,128)} %bitcast.15), calls=%async_computation | async-start | bytes 2097152 | tf_op jit(solution)/shard_map/all_to_all | solution.py:178
  45.5 0.0 collective-permute-done.9
  45.5 2.7 %add.101 = f32[256,1024]{1,0:T(8,128)} add(f32[256,1024]{1,0:T(8,128)} %get-tuple-element.11, f32[256,1024]{1,0:T(8,128)} %collective-permute-done.9) | non-fusion elementwise | flops 262144 | bytes 3145728 | tf_op jit(solution)/shard_map/add | solution.py:195
  48.3 14.3 %all-to-all-done.got_ref = f32[8,32,1024]{2,1,0:T(8,128)S(1)} async-done(((f32[8,32,1024]{2,1,0:T(8,128)}), f32[8,32,1024]{2,1,0:T(8,128)S(1)}, u32[]{:S(2)}, u32[]{:S(2)}) %all-to-all-start) | async-done | bytes 1048608 | tf_op jit(solution)/shard_map/all_to_all | solution.py:178
  62.5 0.0 copy-start.1
  62.5 1.0 copy-done.1
  63.5 3.6 %all-to-all-start.2 = ((f32[8,32,1024]{2,1,0:T(8,128)}), f32[8,32,1024]{2,1,0:T(8,128)S(1)}, u32[]{:S(2)}, u32[]{:S(2)}) async-start(f32[8,32,1024]{2,1,0:T(8,128)} %bitcast.14), calls=%async_computation.2 | async-start | bytes 2097152 | tf_op jit(solution)/shard_map/all_to_all | solution.py:178
  67.1 0.0 copy-start.2
  67.1 1.2 copy-done.2
  68.3 0.4 shard_map.38.refs_0_
  68.7 1.1 collective-permute-start.4
  69.9 2.7 %collective-permute-start.3 = (f32[32,1024]{1,0:T(8,128)S(1)}, f32[32,1024]{1,0:T(8,128)S(1)}, u32[]{:S(2)}, u32[]{:S(2)}) collective-permute-start(f32[32,1024]{1,0:T(8,128)S(1)} %shard_map.38.refs_0_), channel_id=1, source_target_pairs={{0,48},{16,0},{32,16},{48,32},{1,49},{17,1},{33,17},{49,33},{2,50}... | collective-permute-start | bytes 393224 | tf_op jit(solution)/shard_map/ppermute | solution.py:204
  72.6 0.8 collective-permute-start.2
  73.4 0.9 collective-permute-start.1
  74.3 8.3 %collective-permute-done.4.refs_4_ = f32[32,1024]{1,0:T(8,128)S(1)} collective-permute-done((f32[32,1024]{1,0:T(8,128)S(1)}, f32[32,1024]{1,0:T(8,128)S(1)}, u32[]{:S(2)}, u32[]{:S(2)}) %collective-permute-start.4) | collective-permute-done | bytes 131104 | tf_op jit(solution)/shard_map/ppermute | solution.py:199
  82.6 2.7 %collective-permute-start.7 = (f32[32,1024]{1,0:T(8,128)S(1)}, f32[32,1024]{1,0:T(8,128)}, u32[]{:S(2)}, u32[]{:S(2)}) collective-permute-start(f32[32,1024]{1,0:T(8,128)S(1)} %collective-permute-done.4.refs_4_), channel_id=1, source_target_pairs={{0,48},{16,0},{32,16},{48,32},{1,49},{17,1},{33,17},{49,33},{2,50}... | collective-permute-start | bytes 393224 | tf_op jit(solution)/shard_map/ppermute | solution.py:204
  85.4 0.0 collective-permute-done.8.refs_9_
  85.4 0.8 collective-permute-start.6
  86.2 0.0 collective-permute-done.3.refs_3_
  86.2 0.9 collective-permute-start.5
  87.1 0.1 stack.43.place_ref
  87.2 0.0 collective-permute-done.2.refs_2_
  87.2 0.0 collective-permute-done.1.refs_1_
  87.2 2.6 %collective-permute-done.7.refs_7_ = f32[32,1024]{1,0:T(8,128)} collective-permute-done((f32[32,1024]{1,0:T(8,128)S(1)}, f32[32,1024]{1,0:T(8,128)}, u32[]{:S(2)}, u32[]{:S(2)}) %collective-permute-start.7) | collective-permute-done | bytes 131104 | tf_op jit(solution)/shard_map/ppermute | solution.py:204
  89.8 2.4 %collective-permute-done.6.refs_6_ = f32[32,1024]{1,0:T(8,128)} collective-permute-done((f32[32,1024]{1,0:T(8,128)S(1)}, f32[32,1024]{1,0:T(8,128)}, u32[]{:S(2)}, u32[]{:S(2)}) %collective-permute-start.6) | collective-permute-done | bytes 131104 | tf_op jit(solution)/shard_map/ppermute | solution.py:204
  92.2 1.3 collective-permute-done.5.refs_5_
  93.5 4.9 %shard_map.39 = f32[256,1024]{1,0:T(8,128)} custom-call(s32[10]{0:T(128)S(1)} %stack.43.place_ref, f32[32,1024]{1,0:T(8,128)S(1)} %shard_map.38.refs_0_, f32[32,1024]{1,0:T(8,128)} %collective-permute-done.1.refs_1_, f32[32,1024]{1,0:T(8,128)} %collective-permute-done.2.refs_2_, f32[32,1024]{1,0:T(8,128)S(1)} %collective-permute-done.3.refs_3_, ...), custom_call_target="tpu_custom_call" | custom-call | flops 1610612736 | bytes 6291456 | tf_op jit(solution)/shard_map/pallas_call | solution.py:122
  98.4 0.0 all-to-all-done.2.got_ref
  98.4 8.9 %all-to-all-start.1 = ((f32[8,32,1024]{2,1,0:T(8,128)}), f32[8,32,1024]{2,1,0:T(8,128)}, u32[]{:S(2)}, u32[]{:S(2)}) async-start(f32[8,32,1024]{2,1,0:T(8,128)} %bitcast.11), calls=%async_computation.1 | async-start | bytes 2097152 | tf_op jit(solution)/shard_map/all_to_all | solution.py:178
  107.3 0.4 shard_map.41.refs_0_
  107.7 0.1 collective-permute-start.13
  107.8 0.6 collective-permute-start.12
  108.4 0.8 collective-permute-start.11
  109.3 0.9 collective-permute-start.10
  110.1 11.8 %collective-permute-done.13.refs_4_ = f32[32,1024]{1,0:T(8,128)S(1)} collective-permute-done((f32[32,1024]{1,0:T(8,128)S(1)}, f32[32,1024]{1,0:T(8,128)S(1)}, u32[]{:S(2)}, u32[]{:S(2)}) %collective-permute-start.13) | collective-permute-done | bytes 131104 | tf_op jit(solution)/shard_map/ppermute | solution.py:199
  121.9 0.0 collective-permute-start.16
  121.9 0.4 collective-permute-start.15
  122.4 0.0 collective-permute-done.12.refs_3_
  122.4 1.6 collective-permute-start.14
  123.9 0.0 collective-permute-done.11.refs_2_
  123.9 0.0 collective-permute-done.10.refs_1_
  123.9 3.9 %collective-permute-done.16.refs_7_ = f32[32,1024]{1,0:T(8,128)S(1)} collective-permute-done((f32[32,1024]{1,0:T(8,128)S(1)}, f32[32,1024]{1,0:T(8,128)S(1)}, u32[]{:S(2)}, u32[]{:S(2)}) %collective-permute-start.16) | collective-permute-done | bytes 131104 | tf_op jit(solution)/shard_map/ppermute | solution.py:204
  127.8 1.8 %collective-permute-done.15.refs_6_ = f32[32,1024]{1,0:T(8,128)S(1)} collective-permute-done((f32[32,1024]{1,0:T(8,128)S(1)}, f32[32,1024]{1,0:T(8,128)S(1)}, u32[]{:S(2)}, u32[]{:S(2)}) %collective-permute-start.15) | collective-permute-done | bytes 131104 | tf_op jit(solution)/shard_map/ppermute | solution.py:204
  129.6 1.1 collective-permute-done.14.refs_5_
  130.7 4.8 %shard_map.42 = f32[256,1024]{1,0:T(8,128)} custom-call(s32[10]{0:T(128)S(1)} %stack.43.place_ref, f32[32,1024]{1,0:T(8,128)S(1)} %shard_map.41.refs_0_, f32[32,1024]{1,0:T(8,128)S(1)} %collective-permute-done.10.refs_1_, f32[32,1024]{1,0:T(8,128)S(1)} %collective-permute-done.11.refs_2_, f32[32,1024]{1,0:T(8,128)S(1)} %collective-permute-done.12.refs_3_, ...), custom_call_target="tpu_custom_call" | custom-call | flops 1610612736 | bytes 6291456 | tf_op jit(solution)/shard_map/pallas_call | solution.py:122
  135.5 0.0 all-to-all-done.1
  135.5 8.5 %all-to-all-start.3 = ((f32[8,32,1024]{2,1,0:T(8,128)}), f32[8,32,1024]{2,1,0:T(8,128)S(1)}, u32[]{:S(2)}, u32[]{:S(2)}) async-start(f32[8,32,1024]{2,1,0:T(8,128)} %bitcast.13), calls=%async_computation.3 | async-start | bytes 2097152 | tf_op jit(solution)/shard_map/all_to_all | solution.py:178
  143.9 1.3 reduce_sum.9.done_ref
  145.2 15.0 %all-to-all-done.3.got_ref = f32[8,32,1024]{2,1,0:T(8,128)S(1)} async-done(((f32[8,32,1024]{2,1,0:T(8,128)}), f32[8,32,1024]{2,1,0:T(8,128)S(1)}, u32[]{:S(2)}, u32[]{:S(2)}) %all-to-all-start.3) | async-done | bytes 1048608 | tf_op jit(solution)/shard_map/all_to_all | solution.py:178
  160.2 0.8 shard_map.43
Async XLA Ops:
  0.0 17.9 %copy-start = (f32[512,1024]{1,0:T(8,128)S(1)}, f32[512,1024]{1,0:T(8,128)}, u32[]{:S(2)}) copy-start(f32[512,1024]{1,0:T(8,128)} %refs_8_.3) | copy-start | bytes 6291460
  17.8 18.6 %copy-start.3 = (f32[256,1024]{1,0:T(8,128)S(1)}, f32[256,1024]{1,0:T(8,128)}, u32[]{:S(2)}) copy-start(f32[256,1024]{1,0:T(8,128)} %get-tuple-element.9) | copy-start | bytes 3145732
  17.8 18.6 %collective-permute-start = (f32[256,1024]{1,0:T(8,128)S(1)}, f32[256,1024]{1,0:T(8,128)S(1)}, u32[]{:S(2)}, u32[]{:S(2)}) collective-permute-start(f32[256,1024]{1,0:T(8,128)S(1)} %get-tuple-element.10), channel_id=1, source_target_pairs={{0,1},{1,0},{2,3},{3,2},{4,5},{5,4},{6,7},{7,6},{8,9},{9,8},{10,11... | collective-permute-start | bytes 3145736 | tf_op jit(solution)/shard_map/ppermute | solution.py:191
  17.9 67.4 %collective-permute-start.8 = (f32[512,1024]{1,0:T(8,128)S(1)}, f32[512,1024]{1,0:T(8,128)}, u32[]{:S(2)}, u32[]{:S(2)}) collective-permute-start(f32[512,1024]{1,0:T(8,128)S(1)} %copy-done), channel_id=1, source_target_pairs={{0,1},{1,0},{2,3},{3,2},{4,5},{5,4},{6,7},{7,6},{8,9},{9,8},{10,11... | collective-permute-start | bytes 6291464 | tf_op jit(solution)/shard_map/ppermute | solution.py:187
  36.3 9.3 %collective-permute-start.9 = (f32[256,1024]{1,0:T(8,128)}, f32[256,1024]{1,0:T(8,128)}, u32[]{:S(2)}, u32[]{:S(2)}) collective-permute-start(f32[256,1024]{1,0:T(8,128)} %get-tuple-element.12), channel_id=1, source_target_pairs={{0,1},{1,0},{2,3},{3,2},{4,5},{5,4},{6,7},{7,6},{8,9},{9,8},{10,11... | collective-permute-start | bytes 3145736 | tf_op jit(solution)/shard_map/ppermute | solution.py:191
  37.6 24.9 %all-to-all-start = ((f32[8,32,1024]{2,1,0:T(8,128)}), f32[8,32,1024]{2,1,0:T(8,128)S(1)}, u32[]{:S(2)}, u32[]{:S(2)}) async-start(f32[8,32,1024]{2,1,0:T(8,128)} %bitcast.15), calls=%async_computation | async-start | bytes 2097152 | tf_op jit(solution)/shard_map/all_to_all | solution.py:178
  62.5 1.0 copy-start.1
  63.5 34.9 %all-to-all-start.2 = ((f32[8,32,1024]{2,1,0:T(8,128)}), f32[8,32,1024]{2,1,0:T(8,128)S(1)}, u32[]{:S(2)}, u32[]{:S(2)}) async-start(f32[8,32,1024]{2,1,0:T(8,128)} %bitcast.14), calls=%async_computation.2 | async-start | bytes 2097152 | tf_op jit(solution)/shard_map/all_to_all | solution.py:178
  67.1 1.2 copy-start.2
  68.7 13.9 %collective-permute-start.4 = (f32[32,1024]{1,0:T(8,128)S(1)}, f32[32,1024]{1,0:T(8,128)S(1)}, u32[]{:S(2)}, u32[]{:S(2)}) collective-permute-start(f32[32,1024]{1,0:T(8,128)S(1)} %shard_map.38.refs_0_), channel_id=1, source_target_pairs={{0,64},{64,0},{1,65},{65,1},{2,66},{66,2},{3,67},{67,3},{4,68},{68... | collective-permute-start | bytes 393224 | tf_op jit(solution)/shard_map/ppermute | solution.py:199
  69.9 16.3 %collective-permute-start.3 = (f32[32,1024]{1,0:T(8,128)S(1)}, f32[32,1024]{1,0:T(8,128)S(1)}, u32[]{:S(2)}, u32[]{:S(2)}) collective-permute-start(f32[32,1024]{1,0:T(8,128)S(1)} %shard_map.38.refs_0_), channel_id=1, source_target_pairs={{0,48},{16,0},{32,16},{48,32},{1,49},{17,1},{33,17},{49,33},{2,50}... | collective-permute-start | bytes 393224 | tf_op jit(solution)/shard_map/ppermute | solution.py:204
  72.6 14.6 %collective-permute-start.2 = (f32[32,1024]{1,0:T(8,128)S(1)}, f32[32,1024]{1,0:T(8,128)}, u32[]{:S(2)}, u32[]{:S(2)}) collective-permute-start(f32[32,1024]{1,0:T(8,128)S(1)} %shard_map.38.refs_0_), channel_id=1, source_target_pairs={{0,32},{16,48},{32,0},{48,16},{1,33},{17,49},{33,1},{49,17},{2,34}... | collective-permute-start | bytes 393224 | tf_op jit(solution)/shard_map/ppermute | solution.py:204
  73.4 13.7 %collective-permute-start.1 = (f32[32,1024]{1,0:T(8,128)S(1)}, f32[32,1024]{1,0:T(8,128)}, u32[]{:S(2)}, u32[]{:S(2)}) collective-permute-start(f32[32,1024]{1,0:T(8,128)S(1)} %shard_map.38.refs_0_), channel_id=1, source_target_pairs={{0,16},{16,32},{32,48},{48,0},{1,17},{17,33},{33,49},{49,1},{2,18}... | collective-permute-start | bytes 393224 | tf_op jit(solution)/shard_map/ppermute | solution.py:204
  82.6 7.2 %collective-permute-start.7 = (f32[32,1024]{1,0:T(8,128)S(1)}, f32[32,1024]{1,0:T(8,128)}, u32[]{:S(2)}, u32[]{:S(2)}) collective-permute-start(f32[32,1024]{1,0:T(8,128)S(1)} %collective-permute-done.4.refs_4_), channel_id=1, source_target_pairs={{0,48},{16,0},{32,16},{48,32},{1,49},{17,1},{33,17},{49,33},{2,50}... | collective-permute-start | bytes 393224 | tf_op jit(solution)/shard_map/ppermute | solution.py:204
  85.4 6.8 %collective-permute-start.6 = (f32[32,1024]{1,0:T(8,128)S(1)}, f32[32,1024]{1,0:T(8,128)}, u32[]{:S(2)}, u32[]{:S(2)}) collective-permute-start(f32[32,1024]{1,0:T(8,128)S(1)} %collective-permute-done.4.refs_4_), channel_id=1, source_target_pairs={{0,32},{16,48},{32,0},{48,16},{1,33},{17,49},{33,1},{49,17},{2,34}... | collective-permute-start | bytes 393224 | tf_op jit(solution)/shard_map/ppermute | solution.py:204
  86.2 7.3 %collective-permute-start.5 = (f32[32,1024]{1,0:T(8,128)S(1)}, f32[32,1024]{1,0:T(8,128)}, u32[]{:S(2)}, u32[]{:S(2)}) collective-permute-start(f32[32,1024]{1,0:T(8,128)S(1)} %collective-permute-done.4.refs_4_), channel_id=1, source_target_pairs={{0,16},{16,32},{32,48},{48,0},{1,17},{17,33},{33,49},{49,1},{2,18}... | collective-permute-start | bytes 393224 | tf_op jit(solution)/shard_map/ppermute | solution.py:204
  98.4 37.1 %all-to-all-start.1 = ((f32[8,32,1024]{2,1,0:T(8,128)}), f32[8,32,1024]{2,1,0:T(8,128)}, u32[]{:S(2)}, u32[]{:S(2)}) async-start(f32[8,32,1024]{2,1,0:T(8,128)} %bitcast.11), calls=%async_computation.1 | async-start | bytes 2097152 | tf_op jit(solution)/shard_map/all_to_all | solution.py:178
  107.7 14.2 %collective-permute-start.13 = (f32[32,1024]{1,0:T(8,128)S(1)}, f32[32,1024]{1,0:T(8,128)S(1)}, u32[]{:S(2)}, u32[]{:S(2)}) collective-permute-start(f32[32,1024]{1,0:T(8,128)S(1)} %shard_map.41.refs_0_), channel_id=1, source_target_pairs={{0,64},{64,0},{1,65},{65,1},{2,66},{66,2},{3,67},{67,3},{4,68},{68... | collective-permute-start | bytes 393224 | tf_op jit(solution)/shard_map/ppermute | solution.py:199
  107.8 14.6 %collective-permute-start.12 = (f32[32,1024]{1,0:T(8,128)S(1)}, f32[32,1024]{1,0:T(8,128)S(1)}, u32[]{:S(2)}, u32[]{:S(2)}) collective-permute-start(f32[32,1024]{1,0:T(8,128)S(1)} %shard_map.41.refs_0_), channel_id=1, source_target_pairs={{0,48},{16,0},{32,16},{48,32},{1,49},{17,1},{33,17},{49,33},{2,50}... | collective-permute-start | bytes 393224 | tf_op jit(solution)/shard_map/ppermute | solution.py:204
  108.4 15.5 %collective-permute-start.11 = (f32[32,1024]{1,0:T(8,128)S(1)}, f32[32,1024]{1,0:T(8,128)S(1)}, u32[]{:S(2)}, u32[]{:S(2)}) collective-permute-start(f32[32,1024]{1,0:T(8,128)S(1)} %shard_map.41.refs_0_), channel_id=1, source_target_pairs={{0,32},{16,48},{32,0},{48,16},{1,33},{17,49},{33,1},{49,17},{2,34}... | collective-permute-start | bytes 393224 | tf_op jit(solution)/shard_map/ppermute | solution.py:204
  109.3 14.7 %collective-permute-start.10 = (f32[32,1024]{1,0:T(8,128)S(1)}, f32[32,1024]{1,0:T(8,128)S(1)}, u32[]{:S(2)}, u32[]{:S(2)}) collective-permute-start(f32[32,1024]{1,0:T(8,128)S(1)} %shard_map.41.refs_0_), channel_id=1, source_target_pairs={{0,16},{16,32},{32,48},{48,0},{1,17},{17,33},{33,49},{49,1},{2,18}... | collective-permute-start | bytes 393224 | tf_op jit(solution)/shard_map/ppermute | solution.py:204
  121.9 5.9 %collective-permute-start.16 = (f32[32,1024]{1,0:T(8,128)S(1)}, f32[32,1024]{1,0:T(8,128)S(1)}, u32[]{:S(2)}, u32[]{:S(2)}) collective-permute-start(f32[32,1024]{1,0:T(8,128)S(1)} %collective-permute-done.13.refs_4_), channel_id=1, source_target_pairs={{0,48},{16,0},{32,16},{48,32},{1,49},{17,1},{33,17},{49,33},{2,50}... | collective-permute-start | bytes 393224 | tf_op jit(solution)/shard_map/ppermute | solution.py:204
  121.9 7.7 %collective-permute-start.15 = (f32[32,1024]{1,0:T(8,128)S(1)}, f32[32,1024]{1,0:T(8,128)S(1)}, u32[]{:S(2)}, u32[]{:S(2)}) collective-permute-start(f32[32,1024]{1,0:T(8,128)S(1)} %collective-permute-done.13.refs_4_), channel_id=1, source_target_pairs={{0,32},{16,48},{32,0},{48,16},{1,33},{17,49},{33,1},{49,17},{2,34}... | collective-permute-start | bytes 393224 | tf_op jit(solution)/shard_map/ppermute | solution.py:204
  122.4 8.4 %collective-permute-start.14 = (f32[32,1024]{1,0:T(8,128)S(1)}, f32[32,1024]{1,0:T(8,128)S(1)}, u32[]{:S(2)}, u32[]{:S(2)}) collective-permute-start(f32[32,1024]{1,0:T(8,128)S(1)} %collective-permute-done.13.refs_4_), channel_id=1, source_target_pairs={{0,16},{16,32},{32,48},{48,0},{1,17},{17,33},{33,49},{49,1},{2,18}... | collective-permute-start | bytes 393224 | tf_op jit(solution)/shard_map/ppermute | solution.py:204
  135.5 24.7 %all-to-all-start.3 = ((f32[8,32,1024]{2,1,0:T(8,128)}), f32[8,32,1024]{2,1,0:T(8,128)S(1)}, u32[]{:S(2)}, u32[]{:S(2)}) async-start(f32[8,32,1024]{2,1,0:T(8,128)} %bitcast.13), calls=%async_computation.3 | async-start | bytes 2097152 | tf_op jit(solution)/shard_map/all_to_all | solution.py:178

commit v2 on v1

--- a/solution.py
+++ b/solution.py
@@ -94,8 +94,8 @@
 
 
 def cycle_kernel(place_ref, *refs):
-    rows, (w_own, w_far, out_ref), scratch = refs[:8], refs[8:11], refs[11:]
-    half = w_own.shape[0]
+    rows, w, out_ref, scratch = refs[:8], refs[8:12], refs[12], refs[13:]
+    half = w[0].shape[0]
 
     @pl.when(pl.program_id(0) == 0)
     def _():
@@ -109,13 +109,37 @@
 
     own = (scratch[0][...], scratch[1][...])
     far = (scratch[2][...], scratch[3][...])
-    out_ref[...] = product(own, halves(w_own[...]), ((1,), (0,))) + product(
-        far, halves(w_far[...]), ((1,), (0,))
-    )
-
-
-def cycle(place, rows, w_own, w_far):
-    half, columns = w_own.shape
+    out_ref[...] = product(own, (w[0][...], w[1][...]), ((1,), (0,))) + product(
+        far, (w[2][...], w[3][...]), ((1,), (0,))
+    )
+
+
+def split_kernel(own_ref, far_ref, *outs):
+    outs[0][...], outs[1][...] = halves(own_ref[...])
+    outs[2][...], outs[3][...] = halves(far_ref[...])
+
+
+def split_w(own, far):
+    half, columns = own.shape
+    panel = pl.BlockSpec((half, 256), lambda n: (0, n))
+    return pl.pallas_call(
+        split_kernel,
+        out_shape=[jax.ShapeDtypeStruct(own.shape, jnp.bfloat16)] * 4,
+        grid=(columns // 256,),
+        in_specs=[panel] * 2,
+        out_specs=[panel] * 4,
+        compiler_params=pltpu.CompilerParams(
+            dimension_semantics=("arbitrary",), vmem_limit_bytes=16 * 1024 * 1024
+        ),
+        cost_estimate=pl.CostEstimate(
+            flops=4 * own.size, bytes_accessed=16 * own.size, transcendentals=0
+        ),
+        name="split_w",
+    )(own, far)
+
+
+def cycle(place, rows, w):
+    half, columns = w[0].shape
     wide = 512
     whole = pl.BlockSpec(rows[0].shape, lambda n, place: (0, 0))
     panel = pl.BlockSpec((half, wide), lambda n, place: (0, n))
@@ -125,7 +149,7 @@
         grid_spec=pltpu.PrefetchScalarGridSpec(
             num_scalar_prefetch=1,
             grid=(columns // wide,),
-            in_specs=[whole] * 8 + [panel] * 2,
+            in_specs=[whole] * 8 + [panel] * 4,
             out_specs=pl.BlockSpec((8 * O, wide), lambda n, place: (0, n)),
             scratch_shapes=[pltpu.VMEM((8 * O, half), jnp.bfloat16)] * 4,
         ),
@@ -137,7 +161,7 @@
             bytes_accessed=4 * (2 * half * columns + 8 * O * (2 * half + columns)),
             transcendentals=0,
         ),
-    )(place, *rows, w_own, w_far)
+    )(place, *rows, *w)
 
 
 def regroup_kernel(got_ref, out_ref, held):
@@ -185,6 +209,7 @@
         + [core, 1 - core]
     )
     other = lax.ppermute(cycle_inter, "c", SWAP)
+    parts = split_w(cycle_inter, other)
     near, kept = [], []
     for h in range(2):
         far_block, own_block = ladder(core.reshape(1), integrals, amplitudes, h)
@@ -202,7 +227,7 @@
             rows.append(block)
             for step in (1, 2, 3):
                 rows.append(lax.ppermute(block, "x", [(i, (i + step) % 4) for i in range(4)]))
-        part = cycle(place, rows, cycle_inter, other)
+        part = cycle(place, rows, parts)
         got.append(scatter(part.reshape(8, O, part.shape[1])))
     return small(finish_kernel, (2 * O, got[1].shape[2]), [], jnp.sum(got[0], 0), got[1])
 

time: 162 us -> 158 us (0.975)
  waiting for transfers between devices: 62.5 us -> 46.9 us
  starting transfers between devices: 44 us -> 50.9 us
  local copies, waits for them, and re-layouts: 2.27 us -> 5.88 us
  Pallas kernels: 46.9 us -> 48.8 us
    ppermute x12, waiting for transfers between devices: 13.1 us -> 4.01 us  [shards(): lax.ppermute(block, 'x', [(i, (i + step) % 4) for i in range(4)])]
    ppermute x12, starting transfers between devices: 13.2 us -> 21.1 us  [shards(): lax.ppermute(block, 'x', [(i, (i + step) % 4) for i in range(4)])]
    ppermute x2, waiting for transfers between devices: 20.1 us -> 15.1 us  [shards(): far = lax.ppermute(mine, 'zl', SWAP)]
    unnamed x8 -> x14, local copies, waits for them, and re-layouts: 2.19 us -> 5.79 us
    pallas_call x0 -> x1, Pallas kernels: none -> 3.23 us  [split_w(): pl.pallas_call(split_kernel, out_shape=[jax.ShapeDtypeStruct(own.shape, j...]
    pallas_call x2, Pallas kernels: 9.71 us -> 7.14 us  [cycle(): pl.pallas_call(cycle_kernel, out_shape=jax.ShapeDtypeStruct((8 * O, colum...]
  transfers between devices with their start and end apart: 21 -> 21, of which waited for: 10 -> 7; matrix products, arithmetic and copies ran while one was open for 3% -> 3% of each run, Pallas kernels for 18% -> 19%
where the time goes in v2:
time: 158 us
  starting transfers between devices  50.9 us (32%)
  Pallas kernels  48.8 us (31%)
  waiting for transfers between devices  46.9 us (30%)
  local copies, waits for them, and re-layouts  5.88 us (4%)
  other arithmetic  5.18 us (3%)
    pallas_call x2, Pallas kernels, ladder(): pl.pallas_call(functools.partial(ladder_kernel, h), out_shape=[jax.ShapeD...  35.7 us
    all_to_all x4, starting transfers between devices, scatter(): return lax.all_to_all(x, ('y', 'zh'), 0, 0)  27.9 us
    all_to_all x4, waiting for transfers between devices, scatter(): return lax.all_to_all(x, ('y', 'zh'), 0, 0)  27.8 us
    ppermute x12, starting transfers between devices, shards(): lax.ppermute(block, 'x', [(i, (i + step) % 4) for i in range(4)])  21.1 us
    ppermute x2, waiting for transfers between devices, shards(): far = lax.ppermute(mine, 'zl', SWAP)  15.1 us
    pallas_call x2, Pallas kernels, cycle(): pl.pallas_call(cycle_kernel, out_shape=jax.ShapeDtypeStruct((8 * O, colum...  7.14 us
    unnamed x14, local copies, waits for them, and re-layouts  5.79 us
    ppermute x12, waiting for transfers between devices, shards(): lax.ppermute(block, 'x', [(i, (i + step) % 4) for i in range(4)])  4.01 us
  transfers between devices with their start and end apart: 21, of which 7 were waited for; matrix products, arithmetic and copies ran while one was open for 3% of the time, Pallas kernels for 19%

profile of v2, /device:TPU:0, one launch (start us, length us, event | category | flops | bytes accessed | tf_op | source)
XLA Modules:
  0.0 157.8 jit_solution(9980514514859560694)
XLA Ops:
  0.0 17.8 %shard_map.37 = (f32[256,1024]{1,0:T(8,128)S(1)}, f32[256,1024]{1,0:T(8,128)}) custom-call(s32[1]{0:T(128)} %bitcast.8.core_ref, f32[1024,4096]{1,0:T(8,128)} %v_hbm.3, f32[1024,4096]{1,0:T(8,128)} %t_hbm.3), custom_call_target="tpu_custom_call" | custom-call | flops 12884901888 | bytes 25165824 | tf_op jit(solution)/shard_map/pallas_call | solution.py:76
  17.8 0.0 copy-start.6
  17.8 0.1 collective-permute-start
  17.9 0.0 copy-done.4
  17.9 0.5 collective-permute-start.8
  18.4 17.9 %shard_map.40 = (f32[256,1024]{1,0:T(8,128)}, f32[256,1024]{1,0:T(8,128)}) custom-call(s32[1]{0:T(128)} %bitcast.8.core_ref, f32[1024,4096]{1,0:T(8,128)} %v_hbm.3, f32[1024,4096]{1,0:T(8,128)} %t_hbm.3), custom_call_target="tpu_custom_call" | custom-call | flops 12884901888 | bytes 25165824 | tf_op jit(solution)/shard_map/pallas_call | solution.py:76
  36.3 0.2 collective-permute-start.9
  36.5 0.0 collective-permute-done
  36.5 0.0 copy-done.6
  36.5 1.2 add.100
  37.6 7.9 %all-to-all-start = ((f32[8,32,1024]{2,1,0:T(8,128)}), f32[8,32,1024]{2,1,0:T(8,128)S(1)}, u32[]{:S(2)}, u32[]{:S(2)}) async-start(f32[8,32,1024]{2,1,0:T(8,128)} %bitcast.17), calls=%async_computation | async-start | bytes 2097152 | tf_op jit(solution)/shard_map/all_to_all | solution.py:202
  45.5 0.0 collective-permute-done.9
  45.5 2.7 %add.101 = f32[256,1024]{1,0:T(8,128)} add(f32[256,1024]{1,0:T(8,128)} %get-tuple-element.19, f32[256,1024]{1,0:T(8,128)} %collective-permute-done.9) | non-fusion elementwise | flops 262144 | bytes 3145728 | tf_op jit(solution)/shard_map/add | solution.py:220
  48.2 14.4 %all-to-all-done.got_ref = f32[8,32,1024]{2,1,0:T(8,128)S(1)} async-done(((f32[8,32,1024]{2,1,0:T(8,128)}), f32[8,32,1024]{2,1,0:T(8,128)S(1)}, u32[]{:S(2)}, u32[]{:S(2)}) %all-to-all-start) | async-done | bytes 1048608 | tf_op jit(solution)/shard_map/all_to_all | solution.py:202
  62.6 4.2 %all-to-all-start.2 = ((f32[8,32,1024]{2,1,0:T(8,128)}), f32[8,32,1024]{2,1,0:T(8,128)}, u32[]{:S(2)}, u32[]{:S(2)}) async-start(f32[8,32,1024]{2,1,0:T(8,128)} %bitcast.16), calls=%async_computation.2 | async-start | bytes 2097152 | tf_op jit(solution)/shard_map/all_to_all | solution.py:202
  66.9 0.4 shard_map.38.refs_0_
  67.3 1.1 collective-permute-start.4
  68.4 1.5 collective-permute-start.1
  69.9 2.7 %collective-permute-start.2 = (f32[32,1024]{1,0:T(8,128)S(1)}, f32[32,1024]{1,0:T(8,128)}, u32[]{:S(2)}, u32[]{:S(2)}) collective-permute-start(f32[32,1024]{1,0:T(8,128)S(1)} %shard_map.38.refs_0_), channel_id=1, source_target_pairs={{0,32},{16,48},{32,0},{48,16},{1,33},{17,49},{33,1},{49,17},{2,34}... | collective-permute-start | bytes 393224 | tf_op jit(solution)/shard_map/ppermute | solution.py:229
  72.6 1.4 collective-permute-start.3
  74.0 8.2 %collective-permute-done.4.refs_4_ = f32[32,1024]{1,0:T(8,128)S(1)} collective-permute-done((f32[32,1024]{1,0:T(8,128)S(1)}, f32[32,1024]{1,0:T(8,128)S(1)}, u32[]{:S(2)}, u32[]{:S(2)}) %collective-permute-start.4) | collective-permute-done | bytes 131104 | tf_op jit(solution)/shard_map/ppermute | solution.py:224
  82.3 1.5 collective-permute-start.5
  83.7 0.0 collective-permute-done.8.far_ref
  83.8 2.7 %collective-permute-start.6 = (f32[32,1024]{1,0:T(8,128)S(1)}, f32[32,1024]{1,0:T(8,128)}, u32[]{:S(2)}, u32[]{:S(2)}) collective-permute-start(f32[32,1024]{1,0:T(8,128)S(1)} %collective-permute-done.4.refs_4_), channel_id=1, source_target_pairs={{0,32},{16,48},{32,0},{48,16},{1,33},{17,49},{33,1},{49,17},{2,34}... | collective-permute-start | bytes 393224 | tf_op jit(solution)/shard_map/ppermute | solution.py:229
  86.5 0.0 collective-permute-done.1.refs_1_
  86.5 1.4 collective-permute-start.7
  87.9 0.1 stack.43.place_ref
  88.0 1.6 %copy-done.5 = f32[512,1024]{1,0:T(8,128)S(1)} copy-done((f32[512,1024]{1,0:T(8,128)S(1)}, f32[512,1024]{1,0:T(8,128)}, u32[]{:S(2)}) %copy-start.5) | copy-done | bytes 2097176
  89.6 3.2 %split_w.1 = (bf16[512,1024]{1,0:T(8,128)(2,1)S(1)}, bf16[512,1024]{1,0:T(8,128)(2,1)S(1)}, bf16[512,1024]{1,0:T(8,128)(2,1)S(1)}, bf16[512,1024]{1,0:T(8,128)(2,1)S(1)}) custom-call(f32[512,1024]{1,0:T(8,128)S(1)} %copy-done.5, f32[512,1024]{1,0:T(8,128)} %collective-permute-done.8.far_ref), custom_call_target="tpu_custom_call" | custom-call | flops 2097152 | bytes 8388608 | tf_op jit(solution)/shard_map/split_w/pallas_call | solution.py:125
  92.8 0.0 collective-permute-done.2.refs_2_
  92.9 0.0 collective-permute-done.3.refs_3_
  92.9 0.0 collective-permute-done.5.refs_5_
  92.9 0.0 collective-permute-done.6.refs_6_
  92.9 0.0 collective-permute-done.7.refs_7_
  92.9 4.1 %shard_map.39 = f32[256,1024]{1,0:T(8,128)S(1)} custom-call(s32[10]{0:T(128)S(1)} %stack.43.place_ref, f32[32,1024]{1,0:T(8,128)S(1)} %shard_map.38.refs_0_, f32[32,1024]{1,0:T(8,128)S(1)} %collective-permute-done.1.refs_1_, f32[32,1024]{1,0:T(8,128)} %collective-permute-done.2.refs_2_, f32[32,1024]{1,0:T(8,128)} %collective-permute-done.3.refs_3_, ...), custom_call_target="tpu_custom_call" | custom-call | flops 1610612736 | bytes 6291456 | tf_op jit(solution)/shard_map/pallas_call | solution.py:146
  97.0 0.0 copy-start
  97.0 1.0 copy-done
  98.0 1.0 copy-done.2
  99.0 0.0 all-to-all-done.2.got_ref
  99.0 7.4 %all-to-all-start.1 = ((f32[8,32,1024]{2,1,0:T(8,128)}), f32[8,32,1024]{2,1,0:T(8,128)}, u32[]{:S(2)}, u32[]{:S(2)}) async-start(f32[8,32,1024]{2,1,0:T(8,128)} %bitcast.14), calls=%async_computation.1 | async-start | bytes 2097152 | tf_op jit(solution)/shard_map/all_to_all | solution.py:202
  106.4 1.6 %shard_map.41.refs_0_ = f32[32,1024]{1,0:T(8,128)S(1)} custom-call(f32[8,32,1024]{2,1,0:T(8,128)} %all-to-all-done.2.got_ref), custom_call_target="tpu_custom_call" | custom-call | flops 1048576 | bytes 1048576 | tf_op jit(solution)/shard_map/pallas_call | solution.py:190
  108.0 0.1 collective-permute-start.13
  108.1 1.1 collective-permute-start.10
  109.2 2.4 %collective-permute-start.11 = (f32[32,1024]{1,0:T(8,128)S(1)}, f32[32,1024]{1,0:T(8,128)S(1)}, u32[]{:S(2)}, u32[]{:S(2)}) collective-permute-start(f32[32,1024]{1,0:T(8,128)S(1)} %shard_map.41.refs_0_), channel_id=1, source_target_pairs={{0,32},{16,48},{32,0},{48,16},{1,33},{17,49},{33,1},{49,17},{2,34}... | collective-permute-start | bytes 393224 | tf_op jit(solution)/shard_map/ppermute | solution.py:229
  111.6 1.5 collective-permute-start.12
  113.2 6.8 %collective-permute-done.13.refs_4_ = f32[32,1024]{1,0:T(8,128)S(1)} collective-permute-done((f32[32,1024]{1,0:T(8,128)S(1)}, f32[32,1024]{1,0:T(8,128)S(1)}, u32[]{:S(2)}, u32[]{:S(2)}) %collective-permute-start.13) | collective-permute-done | bytes 131104 | tf_op jit(solution)/shard_map/ppermute | solution.py:224
  120.0 1.4 collective-permute-start.14
  121.4 2.4 %collective-permute-start.15 = (f32[32,1024]{1,0:T(8,128)S(1)}, f32[32,1024]{1,0:T(8,128)S(1)}, u32[]{:S(2)}, u32[]{:S(2)}) collective-permute-start(f32[32,1024]{1,0:T(8,128)S(1)} %collective-permute-done.13.refs_4_), channel_id=1, source_target_pairs={{0,32},{16,48},{32,0},{48,16},{1,33},{17,49},{33,1},{49,17},{2,34}... | collective-permute-start | bytes 393224 | tf_op jit(solution)/shard_map/ppermute | solution.py:229
  123.8 0.0 collective-permute-done.10.refs_1_
  123.8 1.0 collective-permute-start.16
  124.7 0.0 collective-permute-done.11.refs_2_
  124.7 0.0 collective-permute-done.12.refs_3_
  124.7 2.4 %collective-permute-done.14.refs_5_ = f32[32,1024]{1,0:T(8,128)S(1)} collective-permute-done((f32[32,1024]{1,0:T(8,128)S(1)}, f32[32,1024]{1,0:T(8,128)S(1)}, u32[]{:S(2)}, u32[]{:S(2)}) %collective-permute-start.14) | collective-permute-done | bytes 131104 | tf_op jit(solution)/shard_map/ppermute | solution.py:229
  127.2 1.4 collective-permute-done.15.refs_6_
  128.6 0.2 collective-permute-done.16.refs_7_
  128.7 1.2 copy-done.1
  130.0 3.1 %shard_map.42 = f32[256,1024]{1,0:T(8,128)S(1)} custom-call(s32[10]{0:T(128)S(1)} %stack.43.place_ref, f32[32,1024]{1,0:T(8,128)S(1)} %shard_map.41.refs_0_, f32[32,1024]{1,0:T(8,128)S(1)} %collective-permute-done.10.refs_1_, f32[32,1024]{1,0:T(8,128)S(1)} %collective-permute-done.11.refs_2_, f32[32,1024]{1,0:T(8,128)S(1)} %collective-permute-done.12.refs_3_, ...), custom_call_target="tpu_custom_call" | custom-call | flops 1610612736 | bytes 6291456 | tf_op jit(solution)/shard_map/pallas_call | solution.py:146
  133.0 0.0 copy-start.3
  133.0 1.0 copy-done.3
  134.0 0.0 all-to-all-done.1
  134.0 8.3 %all-to-all-start.3 = ((f32[8,32,1024]{2,1,0:T(8,128)}), f32[8,32,1024]{2,1,0:T(8,128)S(1)}, u32[]{:S(2)}, u32[]{:S(2)}) async-start(f32[8,32,1024]{2,1,0:T(8,128)} %bitcast.15), calls=%async_computation.3 | async-start | bytes 2097152 | tf_op jit(solution)/shard_map/all_to_all | solution.py:202
  142.4 1.3 reduce_sum.9.done_ref
  143.7 13.4 %all-to-all-done.3.got_ref = f32[8,32,1024]{2,1,0:T(8,128)S(1)} async-done(((f32[8,32,1024]{2,1,0:T(8,128)}), f32[8,32,1024]{2,1,0:T(8,128)S(1)}, u32[]{:S(2)}, u32[]{:S(2)}) %all-to-all-start.3) | async-done | bytes 1048608 | tf_op jit(solution)/shard_map/all_to_all | solution.py:202
  157.1 0.8 shard_map.43
  (4 shorter events, 0.0 us)
Async XLA Ops:
  0.0 17.9 %copy-start.4 = (f32[512,1024]{1,0:T(8,128)S(1)}, f32[512,1024]{1,0:T(8,128)}, u32[]{:S(2)}) copy-start(f32[512,1024]{1,0:T(8,128)} %own_ref.1) | copy-start | bytes 6291460
  17.8 18.6 %copy-start.6 = (f32[256,1024]{1,0:T(8,128)S(1)}, f32[256,1024]{1,0:T(8,128)}, u32[]{:S(2)}) copy-start(f32[256,1024]{1,0:T(8,128)} %get-tuple-element.13) | copy-start | bytes 3145732
  17.8 18.6 %collective-permute-start = (f32[256,1024]{1,0:T(8,128)S(1)}, f32[256,1024]{1,0:T(8,128)S(1)}, u32[]{:S(2)}, u32[]{:S(2)}) collective-permute-start(f32[256,1024]{1,0:T(8,128)S(1)} %get-tuple-element.14), channel_id=1, source_target_pairs={{0,1},{1,0},{2,3},{3,2},{4,5},{5,4},{6,7},{7,6},{8,9},{9,8},{10,11... | collective-permute-start | bytes 3145736 | tf_op jit(solution)/shard_map/ppermute | solution.py:216
  17.9 65.8 %collective-permute-start.8 = (f32[512,1024]{1,0:T(8,128)S(1)}, f32[512,1024]{1,0:T(8,128)}, u32[]{:S(2)}, u32[]{:S(2)}) collective-permute-start(f32[512,1024]{1,0:T(8,128)S(1)} %copy-done.4), channel_id=1, source_target_pairs={{0,1},{1,0},{2,3},{3,2},{4,5},{5,4},{6,7},{7,6},{8,9},{9,8},{10,11... | collective-permute-start | bytes 6291464 | tf_op jit(solution)/shard_map/ppermute | solution.py:211
  36.3 9.3 %collective-permute-start.9 = (f32[256,1024]{1,0:T(8,128)}, f32[256,1024]{1,0:T(8,128)}, u32[]{:S(2)}, u32[]{:S(2)}) collective-permute-start(f32[256,1024]{1,0:T(8,128)} %get-tuple-element.20), channel_id=1, source_target_pairs={{0,1},{1,0},{2,3},{3,2},{4,5},{5,4},{6,7},{7,6},{8,9},{9,8},{10,11... | collective-permute-start | bytes 3145736 | tf_op jit(solution)/shard_map/ppermute | solution.py:216
  37.6 25.0 %all-to-all-start = ((f32[8,32,1024]{2,1,0:T(8,128)}), f32[8,32,1024]{2,1,0:T(8,128)S(1)}, u32[]{:S(2)}, u32[]{:S(2)}) async-start(f32[8,32,1024]{2,1,0:T(8,128)} %bitcast.17), calls=%async_computation | async-start | bytes 2097152 | tf_op jit(solution)/shard_map/all_to_all | solution.py:202
  62.6 36.3 %all-to-all-start.2 = ((f32[8,32,1024]{2,1,0:T(8,128)}), f32[8,32,1024]{2,1,0:T(8,128)}, u32[]{:S(2)}, u32[]{:S(2)}) async-start(f32[8,32,1024]{2,1,0:T(8,128)} %bitcast.16), calls=%async_computation.2 | async-start | bytes 2097152 | tf_op jit(solution)/shard_map/all_to_all | solution.py:202
  67.3 14.9 %collective-permute-start.4 = (f32[32,1024]{1,0:T(8,128)S(1)}, f32[32,1024]{1,0:T(8,128)S(1)}, u32[]{:S(2)}, u32[]{:S(2)}) collective-permute-start(f32[32,1024]{1,0:T(8,128)S(1)} %shard_map.38.refs_0_), channel_id=1, source_target_pairs={{0,64},{64,0},{1,65},{65,1},{2,66},{66,2},{3,67},{67,3},{4,68},{68... | collective-permute-start | bytes 393224 | tf_op jit(solution)/shard_map/ppermute | solution.py:224
  68.4 18.1 %collective-permute-start.1 = (f32[32,1024]{1,0:T(8,128)S(1)}, f32[32,1024]{1,0:T(8,128)S(1)}, u32[]{:S(2)}, u32[]{:S(2)}) collective-permute-start(f32[32,1024]{1,0:T(8,128)S(1)} %shard_map.38.refs_0_), channel_id=1, source_target_pairs={{0,16},{16,32},{32,48},{48,0},{1,17},{17,33},{33,49},{49,1},{2,18}... | collective-permute-start | bytes 393224 | tf_op jit(solution)/shard_map/ppermute | solution.py:229
  69.9 23.0 %collective-permute-start.2 = (f32[32,1024]{1,0:T(8,128)S(1)}, f32[32,1024]{1,0:T(8,128)}, u32[]{:S(2)}, u32[]{:S(2)}) collective-permute-start(f32[32,1024]{1,0:T(8,128)S(1)} %shard_map.38.refs_0_), channel_id=1, source_target_pairs={{0,32},{16,48},{32,0},{48,16},{1,33},{17,49},{33,1},{49,17},{2,34}... | collective-permute-start | bytes 393224 | tf_op jit(solution)/shard_map/ppermute | solution.py:229
  72.6 20.2 %collective-permute-start.3 = (f32[32,1024]{1,0:T(8,128)S(1)}, f32[32,1024]{1,0:T(8,128)}, u32[]{:S(2)}, u32[]{:S(2)}) collective-permute-start(f32[32,1024]{1,0:T(8,128)S(1)} %shard_map.38.refs_0_), channel_id=1, source_target_pairs={{0,48},{16,0},{32,16},{48,32},{1,49},{17,1},{33,17},{49,33},{2,50}... | collective-permute-start | bytes 393224 | tf_op jit(solution)/shard_map/ppermute | solution.py:229
  82.3 10.6 %collective-permute-start.5 = (f32[32,1024]{1,0:T(8,128)S(1)}, f32[32,1024]{1,0:T(8,128)}, u32[]{:S(2)}, u32[]{:S(2)}) collective-permute-start(f32[32,1024]{1,0:T(8,128)S(1)} %collective-permute-done.4.refs_4_), channel_id=1, source_target_pairs={{0,16},{16,32},{32,48},{48,0},{1,17},{17,33},{33,49},{49,1},{2,18}... | collective-permute-start | bytes 393224 | tf_op jit(solution)/shard_map/ppermute | solution.py:229
  83.8 9.1 %collective-permute-start.6 = (f32[32,1024]{1,0:T(8,128)S(1)}, f32[32,1024]{1,0:T(8,128)}, u32[]{:S(2)}, u32[]{:S(2)}) collective-permute-start(f32[32,1024]{1,0:T(8,128)S(1)} %collective-permute-done.4.refs_4_), channel_id=1, source_target_pairs={{0,32},{16,48},{32,0},{48,16},{1,33},{17,49},{33,1},{49,17},{2,34}... | collective-permute-start | bytes 393224 | tf_op jit(solution)/shard_map/ppermute | solution.py:229
  86.5 6.4 %collective-permute-start.7 = (f32[32,1024]{1,0:T(8,128)S(1)}, f32[32,1024]{1,0:T(8,128)}, u32[]{:S(2)}, u32[]{:S(2)}) collective-permute-start(f32[32,1024]{1,0:T(8,128)S(1)} %collective-permute-done.4.refs_4_), channel_id=1, source_target_pairs={{0,48},{16,0},{32,16},{48,32},{1,49},{17,1},{33,17},{49,33},{2,50}... | collective-permute-start | bytes 393224 | tf_op jit(solution)/shard_map/ppermute | solution.py:229
  88.0 1.6 %copy-start.5 = (f32[512,1024]{1,0:T(8,128)S(1)}, f32[512,1024]{1,0:T(8,128)}, u32[]{:S(2)}) copy-start(f32[512,1024]{1,0:T(8,128)} %own_ref.1) | copy-start | bytes 6291460
  97.0 1.0 copy-start
  98.0 1.0 copy-start.2
  99.0 35.0 %all-to-all-start.1 = ((f32[8,32,1024]{2,1,0:T(8,128)}), f32[8,32,1024]{2,1,0:T(8,128)}, u32[]{:S(2)}, u32[]{:S(2)}) async-start(f32[8,32,1024]{2,1,0:T(8,128)} %bitcast.14), calls=%async_computation.1 | async-start | bytes 2097152 | tf_op jit(solution)/shard_map/all_to_all | solution.py:202
  108.0 12.0 %collective-permute-start.13 = (f32[32,1024]{1,0:T(8,128)S(1)}, f32[32,1024]{1,0:T(8,128)S(1)}, u32[]{:S(2)}, u32[]{:S(2)}) collective-permute-start(f32[32,1024]{1,0:T(8,128)S(1)} %shard_map.41.refs_0_), channel_id=1, source_target_pairs={{0,64},{64,0},{1,65},{65,1},{2,66},{66,2},{3,67},{67,3},{4,68},{68... | collective-permute-start | bytes 393224 | tf_op jit(solution)/shard_map/ppermute | solution.py:224
  108.1 15.6 %collective-permute-start.10 = (f32[32,1024]{1,0:T(8,128)S(1)}, f32[32,1024]{1,0:T(8,128)S(1)}, u32[]{:S(2)}, u32[]{:S(2)}) collective-permute-start(f32[32,1024]{1,0:T(8,128)S(1)} %shard_map.41.refs_0_), channel_id=1, source_target_pairs={{0,16},{16,32},{32,48},{48,0},{1,17},{17,33},{33,49},{49,1},{2,18}... | collective-permute-start | bytes 393224 | tf_op jit(solution)/shard_map/ppermute | solution.py:229
  109.2 15.5 %collective-permute-start.11 = (f32[32,1024]{1,0:T(8,128)S(1)}, f32[32,1024]{1,0:T(8,128)S(1)}, u32[]{:S(2)}, u32[]{:S(2)}) collective-permute-start(f32[32,1024]{1,0:T(8,128)S(1)} %shard_map.41.refs_0_), channel_id=1, source_target_pairs={{0,32},{16,48},{32,0},{48,16},{1,33},{17,49},{33,1},{49,17},{2,34}... | collective-permute-start | bytes 393224 | tf_op jit(solution)/shard_map/ppermute | solution.py:229
  111.6 13.1 %collective-permute-start.12 = (f32[32,1024]{1,0:T(8,128)S(1)}, f32[32,1024]{1,0:T(8,128)S(1)}, u32[]{:S(2)}, u32[]{:S(2)}) collective-permute-start(f32[32,1024]{1,0:T(8,128)S(1)} %shard_map.41.refs_0_), channel_id=1, source_target_pairs={{0,48},{16,0},{32,16},{48,32},{1,49},{17,1},{33,17},{49,33},{2,50}... | collective-permute-start | bytes 393224 | tf_op jit(solution)/shard_map/ppermute | solution.py:229
  120.0 7.2 %collective-permute-start.14 = (f32[32,1024]{1,0:T(8,128)S(1)}, f32[32,1024]{1,0:T(8,128)S(1)}, u32[]{:S(2)}, u32[]{:S(2)}) collective-permute-start(f32[32,1024]{1,0:T(8,128)S(1)} %collective-permute-done.13.refs_4_), channel_id=1, source_target_pairs={{0,16},{16,32},{32,48},{48,0},{1,17},{17,33},{33,49},{49,1},{2,18}... | collective-permute-start | bytes 393224 | tf_op jit(solution)/shard_map/ppermute | solution.py:229
  121.4 7.2 %collective-permute-start.15 = (f32[32,1024]{1,0:T(8,128)S(1)}, f32[32,1024]{1,0:T(8,128)S(1)}, u32[]{:S(2)}, u32[]{:S(2)}) collective-permute-start(f32[32,1024]{1,0:T(8,128)S(1)} %collective-permute-done.13.refs_4_), channel_id=1, source_target_pairs={{0,32},{16,48},{32,0},{48,16},{1,33},{17,49},{33,1},{49,17},{2,34}... | collective-permute-start | bytes 393224 | tf_op jit(solution)/shard_map/ppermute | solution.py:229
  123.8 5.0 %collective-permute-start.16 = (f32[32,1024]{1,0:T(8,128)S(1)}, f32[32,1024]{1,0:T(8,128)S(1)}, u32[]{:S(2)}, u32[]{:S(2)}) collective-permute-start(f32[32,1024]{1,0:T(8,128)S(1)} %collective-permute-done.13.refs_4_), channel_id=1, source_target_pairs={{0,48},{16,0},{32,16},{48,32},{1,49},{17,1},{33,17},{49,33},{2,50}... | collective-permute-start | bytes 393224 | tf_op jit(solution)/shard_map/ppermute | solution.py:229
  128.7 1.2 copy-start.1
  133.0 1.0 copy-start.3
  134.0 23.0 %all-to-all-start.3 = ((f32[8,32,1024]{2,1,0:T(8,128)}), f32[8,32,1024]{2,1,0:T(8,128)S(1)}, u32[]{:S(2)}, u32[]{:S(2)}) async-start(f32[8,32,1024]{2,1,0:T(8,128)} %bitcast.15), calls=%async_computation.3 | async-start | bytes 2097152 | tf_op jit(solution)/shard_map/all_to_all | solution.py:202
